TPU v7x, 512 devices: a whole 4x4x16 slice. The times are simulated.
512 devices in a mesh: rows: 64 (over y, z), cols: 8 (over x, core).
Axes of the slice: x: 4, y: 4, z: 16, core: 2. Of those that a mesh axis runs over, the one named last changes fastest.
Arguments:
- node_features: bfloat16 [65536, 512], P('rows', 'cols'), may hold values from -6 to 6
- weight: bfloat16 [512, 512], replicated, may hold values from -0.25 to 0.25
- tile_values: bfloat16 [4096, 128, 128], P('rows'), may hold values from -0.1875 to 0.1875
- tile_row: int32 [4096], P('rows'), may hold values from 0 to 7
- source_owner: int32 [4096, 1], P('rows'), may hold values from 0 to 63; in each aligned block of 64 rows (0 to 63, 64 to 127, ...) at most 2 rows name the same one
- source_block: int32 [4096], P('rows'), may hold values from 0 to 7
- labels: int32 [65536], P('rows'), may hold values from 0 to 511
Outputs:
- activations: bfloat16 [65536, 512], P('rows', 'cols')
- weight_grad: float32 [512, 512], P(None, 'cols')
- feature_grad: bfloat16 [65536, 512], P('rows', 'cols')
Inputs may be any that keep to these rules, and one draw needn't show every extreme that they name: `source_owner`: of the 64 tiles of one index of rows, at most 2 name the same owner.
All inputs are finite; a program needn't handle non-finite values.
Results may differ from a plain program's by a relative error of at most 0.0095.
Values may be sent and summed in bfloat16 or wider, within the bound.
A program may use at most 64 MiB of HBM per device.

v0:
```python
import math
import jax
import jax.numpy as jnp
from jax import lax
from jax.sharding import PartitionSpec as P


def slot_ranks(owners):
    positions = jnp.arange(owners.shape[0], dtype=jnp.int32)
    earlier = (owners[:, None] == owners[None, :]) & (positions[None, :] < positions[:, None])
    return jnp.sum(earlier.astype(jnp.int32), axis=1)


def per_device(node_features, weight, tile_values, tile_row, source_owner, source_block, labels):
    local_rows, col_width = node_features.shape
    block_size = tile_values.shape[1]
    local_blocks = local_rows // block_size
    row_devices = lax.axis_size("rows")
    capacity = 2 * tile_values.shape[0] // row_devices
    owners = source_owner[:, 0]
    slot_rank = slot_ranks(owners)
    column_block = owners * local_blocks + source_block
    local_ids = jnp.arange(local_blocks, dtype=jnp.int32)
    row_onehot = (tile_row[:, None] == local_ids[None, :]).astype(jnp.float32)
    gathered = lax.all_gather(node_features, "rows", axis=0, tiled=True)
    all_blocks = gathered.reshape(row_devices * local_blocks, block_size, col_width)
    source_rows = all_blocks[column_block]
    products = jnp.einsum(
        "tij,tjf->tif", tile_values, source_rows, preferred_element_type=jnp.float32
    )
    summed = jnp.einsum("tb,tif->bif", row_onehot, products, precision=lax.Precision.HIGHEST)
    aggregated = summed.reshape(local_rows, col_width).astype(jnp.bfloat16)
    aggregated_all = lax.all_gather(aggregated, "cols", axis=1, tiled=True)
    col_index = lax.axis_index("cols")
    w_columns = lax.dynamic_slice_in_dim(weight, col_index * col_width, col_width, 1)
    w_rows = lax.dynamic_slice_in_dim(weight, col_index * col_width, col_width, 0)
    hidden = jnp.dot(aggregated_all, w_columns, preferred_element_type=jnp.float32)
    sigmoid = jax.nn.sigmoid(hidden)
    activated = hidden * sigmoid
    slopes = sigmoid * (1.0 + hidden * (1.0 - sigmoid))
    feature_ids = col_index * col_width + jnp.arange(col_width, dtype=jnp.int32)
    target = (labels[:, None] == feature_ids[None, :]).astype(jnp.float32)
    out_grad = ((activated - target) * slopes).astype(jnp.bfloat16)
    grad_all = lax.all_gather(out_grad, "cols", axis=1, tiled=True)
    weight_terms = jnp.einsum(
        "nk,nc->kc", aggregated_all, out_grad, preferred_element_type=jnp.float32
    )
    node_total = local_rows * row_devices
    weight_grad = lax.psum(weight_terms, "rows") / math.sqrt(node_total)
    agg_grad = jnp.einsum("nc,kc->nk", grad_all, w_rows, preferred_element_type=jnp.float32).astype(
        jnp.bfloat16
    )
    grad_rows = agg_grad.reshape(local_blocks, block_size, col_width)[tile_row]
    sent_terms = jnp.einsum(
        "tji,tjf->tif", tile_values, grad_rows, preferred_element_type=jnp.float32
    )
    send_terms = (
        jnp.zeros((row_devices, capacity, block_size, col_width), jnp.float32)
        .at[owners, slot_rank]
        .set(sent_terms)
    )
    send_index = (
        jnp.zeros((row_devices, capacity), jnp.int32).at[owners, slot_rank].set(source_block)
    )
    received, recv_index = (
        lax.all_to_all(
            send_terms.astype(jnp.bfloat16), "rows", split_axis=0, concat_axis=0, tiled=True
        ).astype(send_terms.dtype),
        lax.all_to_all(send_index, "rows", split_axis=0, concat_axis=0, tiled=True),
    )
    placing = (recv_index[:, :, None] == local_ids[None, None, :]).astype(jnp.float32)
    filled = (jnp.abs(received).sum(axis=(2, 3)) >= 0.0).astype(jnp.float32)
    feature_grad = jnp.einsum(
        "scb,scif->bif", placing * filled[:, :, None], received, precision=lax.Precision.HIGHEST
    ).reshape(local_rows, col_width)
    return (activated.astype(jnp.bfloat16), weight_grad, feature_grad.astype(jnp.bfloat16))


def solution(mesh):
    return jax.shard_map(
        per_device,
        mesh=mesh,
        in_specs=(
            P("rows", "cols"),
            P(),
            P("rows", None, None),
            P("rows"),
            P("rows", None),
            P("rows"),
            P("rows"),
        ),
        out_specs=(P("rows", "cols"), P(None, "cols"), P("rows", "cols")),
        check_vma=False,
    )
```

profile of v0, /device:TPU:2, one launch (start us, length us, event | category | flops | bytes accessed | tf_op | source)
XLA Modules:
  0.0 590.2 jit_solution(7779311799218977783)
XLA Ops:
  7.2 0.0 copy-start
  7.2 0.0 all-gather.4.cloned.1.call-start
  7.2 0.7 all-gather.4.cloned.1.call-update
  7.9 0.0 all-gather.6.cloned.1.call-start
  8.0 0.7 compare_select_fusion.3
  8.6 164.2 %all-gather.4.cloned.1.call-done = bf16[65536,64]{0,1:T(8,128)(2,1)} async-done(((bf16[1024,64]{0,1:T(8,128)(2,1)}), bf16[65536,64]{0,1:T(8,128)(2,1)}) %all-gather.4.cloned.1.call-update) | async-done | bytes 8388624 | tf_op jit(solution)/shard_map/all_gather | solution.py:25
  172.9 9.0 %copy_bitcast_fusion = bf16[512,128,64]{1,2,0:T(8,128)(2,1)} fusion(bf16[65536,64]{0,1:T(8,128)(2,1)} %all-gather.4.cloned.1.call-done), kind=kLoop, calls=%fused_computation.4 | loop fusion | bytes 16777216 | tf_op jit(solution)/shard_map/reshape | solution.py:26
  181.9 4.1 gather_fusion
  186.0 0.0 copy-done
  186.0 0.0 copy-start.4
  186.0 1.5 convolution_bitcast_fusion.1
  187.6 0.0 copy-done.4
  187.6 0.0 copy-start.5
  187.6 2.0 fusion.10
  189.6 0.0 copy-start.6
  189.6 0.0 copy-start.3
  189.6 0.7 copy.68
  190.3 0.0 all-gather.6.cloned.1.call-update
  190.3 0.0 all-gather.8.cloned.1.call-start
  190.4 24.7 %all-gather.6.cloned.1.call-done = bf16[1024,512]{0,1:T(8,128)(2,1)} async-done(((bf16[1024,64]{0,1:T(8,128)(2,1)}), bf16[1024,512]{0,1:T(8,128)(2,1)}) %all-gather.6.cloned.1.call-update) | async-done | bytes 1048592 | tf_op jit(solution)/shard_map/all_gather | solution.py:33
  215.0 0.0 copy-done.5
  215.0 2.4 multiply_convert_fusion
  217.4 0.0 all-gather.8.cloned.1.call-update
  217.4 0.0 copy-done.6
  217.5 0.2 convert_reduce_fusion
  217.7 0.0 copy-done.3
  217.7 3.5 scatter_fusion
  221.2 0.7 copy.42
  221.9 15.2 %all-to-all-start = ((s32[64,1,2]{2,1,0:T(1,128)}), s32[64,1,2]{2,1,0:T(1,128)S(1)}, u32[]{:S(2)}, u32[]{:S(2)}) async-start(s32[64,1,2]{2,1,0:T(1,128)} %copy.42), calls=%async_computation | async-start | bytes 65536 | tf_op jit(solution)/shard_map/all_to_all | solution.py:69
  237.1 11.6 %all-gather.8.cloned.1.call-done = bf16[1024,512]{0,1:T(8,128)(2,1)} async-done(((bf16[1024,64]{0,1:T(8,128)(2,1)}), bf16[1024,512]{0,1:T(8,128)(2,1)}) %all-gather.8.cloned.1.call-update) | async-done | bytes 1048592 | tf_op jit(solution)/shard_map/all_gather | solution.py:44
  248.7 1.6 fusion.13
  250.3 0.8 gather_fusion.1
  251.1 2.0 convolution_bitcast_fusion
  253.1 2.5 broadcast_in_dim.10
  255.6 10.6 %scatter_fusion.1 = f32[64,2,128,64]{2,3,1,0:T(8,128)} fusion(f32[64,2,128,64]{2,3,1,0:T(8,128)} %broadcast_in_dim.10, s32[64]{0:T(128)S(1)} %fusion.31, f32[64,128,64]{1,2,0:T(8,128)} %convolution_bitcast_fusion), kind=kCustom, calls=%fused_computation.3 | custom fusion | bytes 6291968 | tf_op jit(solution)/shard_map/scatter | solution.py:60
  266.2 2.7 convert_element_type.49
  268.9 3.5 copy.45
  272.4 0.0 copy-start.1
  272.4 0.0 copy-start.2
  272.4 0.0 all-to-all-done
  272.4 15.9 %all-to-all-start.1 = ((bf16[64,2,128,64]{2,1,3,0:T(2,128)(2,1)}), bf16[64,2,128,64]{2,1,3,0:T(2,128)(2,1)}, u32[]{:S(2)}, u32[]{:S(2)}) async-start(bf16[64,2,128,64]{2,1,3,0:T(2,128)(2,1)} %copy.45), calls=%async_computation.1 | async-start | bytes 4194304 | tf_op jit(solution)/shard_map/all_to_all | solution.py:66
  288.4 0.0 all-reduce.2.cloned.1.call-start
  288.4 0.0 copy-done.1
  288.4 0.0 copy-done.2
  288.4 1.1 fusion.33
  289.5 0.0 all-reduce.2.cloned.1.call-update
  289.6 0.1 copy.43
  289.6 283.3 %all-reduce.2.cloned.1.call-done = f32[512,64]{0,1:T(8,128)} async-done(((f32[512,64]{0,1:T(8,128)}), f32[512,64]{0,1:T(8,128)}) %all-reduce.2.cloned.1.call-update) | async-done | bytes 131088 | tf_op jit(solution)/shard_map/psum | solution.py:49
  573.0 1.6 broadcast_multiply_fusion
  574.5 0.0 all-to-all-done.1
  574.5 3.8 abs_reduce_fusion
  578.4 0.1 copy.46
  578.5 4.5 fusion.7
  583.0 0.7 copy.67
  (8 shorter events, 0.1 us)
Async XLA Ops:
  7.2 178.9 %copy-start = (bf16[64,128,128]{2,1,0:T(8,128)(2,1)S(1)}, bf16[64,128,128]{2,1,0:T(8,128)(2,1)}, u32[]{:S(2)}) copy-start(bf16[64,128,128]{2,1,0:T(8,128)(2,1)} %param.9) | copy-start | bytes 6291460
  7.2 165.7 %all-gather.4.cloned.1.call-start = ((), (), s32[]{:S(2)}) async-start(), calls=%async_computation.2 | async-start | bytes 8519680 | tf_op jit(solution)/shard_map/all_gather | solution.py:25
  7.9 207.1 %all-gather.6.cloned.1.call-start = ((), (), s32[]{:S(2)}) async-start(), calls=%async_computation.3 | async-start | bytes 1179648 | tf_op jit(solution)/shard_map/all_gather | solution.py:33
  186.0 1.5 copy-start.4
  187.6 27.4 %copy-start.5 = (s32[1024]{0:T(1024)S(1)}, s32[1024]{0:T(1024)}, u32[]{:S(2)}) copy-start(s32[1024]{0:T(1024)} %param.13) | copy-start | bytes 12292
  189.6 27.9 %copy-start.6 = (s32[64,1]{0,1:T(1,128)S(1)}, s32[64,1]{0,1:T(1,128)}, u32[]{:S(2)}) copy-start(s32[64,1]{0,1:T(1,128)} %param.11) | copy-start | bytes 772
  189.6 28.1 %copy-start.3 = (s32[64]{0:T(128)S(1)}, s32[64]{0:T(128)}, u32[]{:S(2)}) copy-start(s32[64]{0:T(128)} %param.12) | copy-start | bytes 772
  190.3 58.4 %all-gather.8.cloned.1.call-start = ((), (), s32[]{:S(2)}) async-start(), calls=%async_computation.5 | async-start | bytes 1179648 | tf_op jit(solution)/shard_map/all_gather | solution.py:44
  221.9 50.5 %all-to-all-start = ((s32[64,1,2]{2,1,0:T(1,128)}), s32[64,1,2]{2,1,0:T(1,128)S(1)}, u32[]{:S(2)}, u32[]{:S(2)}) async-start(s32[64,1,2]{2,1,0:T(1,128)} %copy.42), calls=%async_computation | async-start | bytes 65536 | tf_op jit(solution)/shard_map/all_to_all | solution.py:69
  272.4 16.0 %copy-start.1 = (bf16[1024,512]{0,1:T(8,128)(2,1)S(1)}, bf16[1024,512]{0,1:T(8,128)(2,1)}, u32[]{:S(2)}) copy-start(bf16[1024,512]{0,1:T(8,128)(2,1)} %all-gather.6.cloned.1.call-done) | copy-start | bytes 3145732
  272.4 16.0 %copy-start.2 = (bf16[1024,64]{0,1:T(8,128)(2,1)S(1)}, bf16[1024,64]{0,1:T(8,128)(2,1)}, u32[]{:S(2)}) copy-start(bf16[1024,64]{0,1:T(8,128)(2,1)} %get-tuple-element.3) | copy-start | bytes 393220
  272.4 302.1 %all-to-all-start.1 = ((bf16[64,2,128,64]{2,1,3,0:T(2,128)(2,1)}), bf16[64,2,128,64]{2,1,3,0:T(2,128)(2,1)}, u32[]{:S(2)}, u32[]{:S(2)}) async-start(bf16[64,2,128,64]{2,1,3,0:T(2,128)(2,1)} %copy.45), calls=%async_computation.1 | async-start | bytes 4194304 | tf_op jit(solution)/shard_map/all_to_all | solution.py:66
  288.4 284.6 %all-reduce.2.cloned.1.call-start = ((), (), s32[]{:S(2)}) async-start(), calls=%async_computation.4 | async-start | bytes 262144 | tf_op jit(solution)/shard_map/psum | solution.py:49
Sparse Core Ops, SparseCore 0:
  11.0 161.8 all-gather.3
  190.4 24.5 all-gather.5
  217.7 30.9 all-gather.7
  292.9 280.0 all-reduce.1
where the time goes:
time: 591 us; the launch traced here: 590 us
  waiting for transfers between devices  485 us (82%)
  local copies, waits for them, and re-layouts  36.3 us (6%)
  starting transfers between devices  31.3 us (5%)
  matrix products  15.1 us (3%)
  between operations  14 us (2%)
  other arithmetic  9.01 us (2%)
    psum x1, waiting for transfers between devices, per_device(): weight_grad = lax.psum(weight_terms, 'rows') / math.sqrt(node_total)  283 us
    all_gather x1, waiting for transfers between devices, per_device(): gathered = lax.all_gather(node_features, 'rows', axis=0, tiled=True)  164 us
    all_gather x1, waiting for transfers between devices, per_device(): aggregated_all = lax.all_gather(aggregated, 'cols', axis=1, tiled=True)  24.7 us
    all_to_all x1, starting transfers between devices, per_device(): lax.all_to_all(send_terms.astype(jnp.bfloat16), 'rows', split_axis=0, con...  15.9 us
    all_to_all x1, starting transfers between devices, per_device(): lax.all_to_all(send_index, 'rows', split_axis=0, concat_axis=0, tiled=True)  15.2 us
  transfers between devices with their start and end apart: 6, of which 4 were waited for; matrix products, arithmetic and copies ran while one was open for 5% of the time, Pallas kernels for 0%

commit v1 on v0

--- a/solution.py
+++ b/solution.py
@@ -22,7 +22,9 @@
     column_block = owners * local_blocks + source_block
     local_ids = jnp.arange(local_blocks, dtype=jnp.int32)
     row_onehot = (tile_row[:, None] == local_ids[None, :]).astype(jnp.float32)
-    gathered = lax.all_gather(node_features, "rows", axis=0, tiled=True)
+    gathered = jnp.concatenate(
+        lax.all_to_all(jnp.stack([node_features] * lax.axis_size("rows")), "rows", 0, 0), axis=0
+    )
     all_blocks = gathered.reshape(row_devices * local_blocks, block_size, col_width)
     source_rows = all_blocks[column_block]
     products = jnp.einsum(

time: 591 us -> 844 us (1.43)
  waiting for transfers between devices: 485 us -> 686 us
  local copies, waits for them, and re-layouts: 36.3 us -> 69.5 us
  starting transfers between devices: 31.3 us -> 50.4 us
    all_to_all x0 -> x1, waiting for transfers between devices: none -> 368 us  [per_device(): lax.all_to_all(jnp.stack([node_features] * lax.axis_size('rows')), 'rows'...]
    all_gather x1 -> x0, waiting for transfers between devices: 164 us -> none  [per_device(): gathered = lax.all_gather(node_features, 'rows', axis=0, tiled=True)]
    another operation x0 -> x3, local copies, waits for them, and re-layouts: none -> 30.8 us  [the longest x2 25.4 us: per_device(): gathered.reshape(row_devices * local_blocks, block_size, col_width)]
    all_to_all x0 -> x1, starting transfers between devices: none -> 19.1 us  [per_device(): lax.all_to_all(jnp.stack([node_features] * lax.axis_size('rows')), 'rows'...]
    all_to_all x0 -> x1, local copies, waits for them, and re-layouts: none -> 11.3 us  [per_device(): lax.all_to_all(jnp.stack([node_features] * lax.axis_size('rows')), 'rows'...]
    reshape x1 -> x0, local copies, waits for them, and re-layouts: 9.04 us -> none  [per_device(): gathered.reshape(row_devices * local_blocks, block_size, col_width)]
  transfers between devices with their start and end apart: 6 -> 6, of which waited for: 4 -> 4; matrix products, arithmetic and copies ran while one was open for 5% -> 4% of each run, Pallas kernels for 0% -> 0%
where the time goes in v1:
time: 844 us; the launch traced here: 843 us
  waiting for transfers between devices  686 us (81%)
  local copies, waits for them, and re-layouts  69.5 us (8%)
  starting transfers between devices  50.4 us (6%)
  matrix products  15.1 us (2%)
  between operations  13.9 us (2%)
    all_to_all x1, waiting for transfers between devices, per_device(): lax.all_to_all(jnp.stack([node_features] * lax.axis_size('rows')), 'rows'...  368 us
    psum x1, waiting for transfers between devices, per_device(): weight_grad = lax.psum(weight_terms, 'rows') / math.sqrt(node_total)  284 us
    another operation x2, local copies, waits for them, and re-layouts, per_device(): gathered.reshape(row_devices * local_blocks, block_size, col_width)  25.4 us
    all_gather x1, waiting for transfers between devices, per_device(): aggregated_all = lax.all_gather(aggregated, 'cols', axis=1, tiled=True)  23 us
    all_to_all x1, starting transfers between devices, per_device(): lax.all_to_all(jnp.stack([node_features] * lax.axis_size('rows')), 'rows'...  19.1 us
  transfers between devices with their start and end apart: 6, of which 4 were waited for; matrix products, arithmetic and copies ran while one was open for 4% of the time, Pallas kernels for 0%

profile of v1, /device:TPU:2, one launch (start us, length us, event | category | flops | bytes accessed | tf_op | source)
XLA Modules:
  0.0 843.3 jit_solution(3870111000933753153)
XLA Ops:
  7.2 0.0 copy-start
  7.2 5.4 stack.2
  12.5 0.0 copy-start.3
  12.5 0.0 copy-start.6
  12.5 19.1 %all-to-all-start = ((bf16[64,1024,64]{1,2,0:T(8,128)(2,1)}), bf16[64,1024,64]{1,2,0:T(8,128)(2,1)}, u32[]{:S(2)}, u32[]{:S(2)}) async-start(bf16[64,1024,64]{1,2,0:T(8,128)(2,1)} %stack.2), calls=%async_computation | async-start | bytes 16777216 | tf_op jit(solution)/shard_map/all_to_all | solution.py:26
  31.7 0.0 all-gather.3.cloned.1.call-start
  31.7 0.0 copy-done.3
  31.7 0.0 copy-done.6
  31.8 367.6 %all-to-all-done = bf16[64,1024,64]{1,2,0:T(8,128)(2,1)} async-done(((bf16[64,1024,64]{1,2,0:T(8,128)(2,1)}), bf16[64,1024,64]{1,2,0:T(8,128)(2,1)}, u32[]{:S(2)}, u32[]{:S(2)}) %all-to-all-start) | async-done | bytes 8388640 | tf_op jit(solution)/shard_map/all_to_all | solution.py:26
  399.4 11.3 %copy.47 = bf16[64,1024,64]{1,0,2:T(8,128)(2,1)} copy(bf16[64,1024,64]{1,2,0:T(8,128)(2,1)} %all-to-all-done) | data formatting | bytes 16777216 | tf_op jit(solution)/shard_map/all_to_all | solution.py:26
  410.7 13.4 %reshape_reshape.3 = bf16[512,128,64]{1,0,2:T(8,128)(2,1)} reshape(bf16[64,1024,64]{1,0,2:T(8,128)(2,1)} %copy.47) | data formatting | bytes 16777216 | tf_op jit(solution)/shard_map/reshape;reshape | solution.py:28
  424.1 12.0 %copy.48 = bf16[512,128,64]{1,2,0:T(8,128)(2,1)} copy(bf16[512,128,64]{1,0,2:T(8,128)(2,1)} %reshape_reshape.3) | data formatting | bytes 16777216 | tf_op jit(solution)/shard_map/reshape;reshape | solution.py:28
  436.1 4.1 gather_fusion
  440.3 0.0 copy-done
  440.3 0.0 copy-start.4
  440.3 1.5 convolution_bitcast_fusion.1
  441.8 0.0 copy-done.4
  441.8 0.0 copy-start.5
  441.8 2.0 fusion.10
  443.8 0.7 copy.74
  444.5 0.0 all-gather.3.cloned.1.call-update
  444.5 0.0 all-gather.5.cloned.1.call-start
  444.6 23.0 %all-gather.3.cloned.1.call-done = bf16[1024,512]{0,1:T(8,128)(2,1)} async-done(((bf16[1024,64]{0,1:T(8,128)(2,1)}), bf16[1024,512]{0,1:T(8,128)(2,1)}) %all-gather.3.cloned.1.call-update) | async-done | bytes 1048592 | tf_op jit(solution)/shard_map/all_gather | solution.py:35
  467.6 0.0 copy-done.5
  467.6 2.4 multiply_convert_fusion
  470.0 0.0 all-gather.5.cloned.1.call-update
  470.1 0.2 convert_reduce_fusion
  470.3 3.5 scatter_fusion
  473.8 0.7 copy.50
  474.5 15.4 %all-to-all-start.1 = ((s32[64,1,2]{2,1,0:T(1,128)}), s32[64,1,2]{2,1,0:T(1,128)S(1)}, u32[]{:S(2)}, u32[]{:S(2)}) async-start(s32[64,1,2]{2,1,0:T(1,128)} %copy.50), calls=%async_computation.1 | async-start | bytes 65536 | tf_op jit(solution)/shard_map/all_to_all | solution.py:71
  489.9 11.4 %all-gather.5.cloned.1.call-done = bf16[1024,512]{0,1:T(8,128)(2,1)} async-done(((bf16[1024,64]{0,1:T(8,128)(2,1)}), bf16[1024,512]{0,1:T(8,128)(2,1)}) %all-gather.5.cloned.1.call-update) | async-done | bytes 1048592 | tf_op jit(solution)/shard_map/all_gather | solution.py:46
  501.3 1.6 fusion.13
  502.9 0.7 gather_fusion.1
  503.7 2.0 convolution_bitcast_fusion
  505.7 2.5 broadcast_in_dim.10
  508.2 10.8 %scatter_fusion.1 = f32[64,2,128,64]{2,3,1,0:T(8,128)} fusion(f32[64,2,128,64]{2,3,1,0:T(8,128)} %broadcast_in_dim.10, s32[64]{0:T(128)S(1)} %fusion.31, f32[64,128,64]{1,2,0:T(8,128)} %convolution_bitcast_fusion), kind=kCustom, calls=%fused_computation.3 | custom fusion | bytes 6291968 | tf_op jit(solution)/shard_map/scatter | solution.py:62
  519.0 2.7 convert_element_type.49
  521.7 3.5 copy.53
  525.1 0.0 copy-start.1
  525.1 0.0 copy-start.2
  525.2 0.0 all-to-all-done.1
  525.2 15.7 %all-to-all-start.2 = ((bf16[64,2,128,64]{2,1,3,0:T(2,128)(2,1)}), bf16[64,2,128,64]{2,1,3,0:T(2,128)(2,1)}, u32[]{:S(2)}, u32[]{:S(2)}) async-start(bf16[64,2,128,64]{2,1,3,0:T(2,128)(2,1)} %copy.53), calls=%async_computation.2 | async-start | bytes 4194304 | tf_op jit(solution)/shard_map/all_to_all | solution.py:68
  540.9 0.0 all-reduce.2.cloned.1.call-start
  541.0 0.0 copy-done.1
  541.0 0.0 copy-done.2
  541.0 1.1 fusion.33
  542.1 0.0 all-reduce.2.cloned.1.call-update
  542.1 0.1 copy.51
  542.2 283.8 %all-reduce.2.cloned.1.call-done = f32[512,64]{0,1:T(8,128)} async-done(((f32[512,64]{0,1:T(8,128)}), f32[512,64]{0,1:T(8,128)}) %all-reduce.2.cloned.1.call-update) | async-done | bytes 131088 | tf_op jit(solution)/shard_map/psum | solution.py:51
  826.0 1.6 broadcast_multiply_fusion
  827.6 0.0 all-to-all-done.2
  827.6 3.8 abs_reduce_fusion
  831.4 0.1 copy.54
  831.5 4.5 fusion.7
  836.1 0.7 copy.73
  (9 shorter events, 0.1 us)
Async XLA Ops:
  7.2 433.1 %copy-start = (bf16[64,128,128]{2,1,0:T(8,128)(2,1)S(1)}, bf16[64,128,128]{2,1,0:T(8,128)(2,1)}, u32[]{:S(2)}) copy-start(bf16[64,128,128]{2,1,0:T(8,128)(2,1)} %param.9) | copy-start | bytes 6291460
  12.5 19.2 %copy-start.3 = (s32[64]{0:T(128)S(1)}, s32[64]{0:T(128)}, u32[]{:S(2)}) copy-start(s32[64]{0:T(128)} %param.12) | copy-start | bytes 772
  12.5 19.2 %copy-start.6 = (s32[64,1]{0,1:T(1,128)S(1)}, s32[64,1]{0,1:T(1,128)}, u32[]{:S(2)}) copy-start(s32[64,1]{0,1:T(1,128)} %param.11) | copy-start | bytes 772
  12.5 386.9 %all-to-all-start = ((bf16[64,1024,64]{1,2,0:T(8,128)(2,1)}), bf16[64,1024,64]{1,2,0:T(8,128)(2,1)}, u32[]{:S(2)}, u32[]{:S(2)}) async-start(bf16[64,1024,64]{1,2,0:T(8,128)(2,1)} %stack.2), calls=%async_computation | async-start | bytes 16777216 | tf_op jit(solution)/shard_map/all_to_all | solution.py:26
  31.7 435.9 %all-gather.3.cloned.1.call-start = ((), (), s32[]{:S(2)}) async-start(), calls=%async_computation.3 | async-start | bytes 1179648 | tf_op jit(solution)/shard_map/all_gather | solution.py:35
  440.3 1.5 copy-start.4
  441.8 25.8 %copy-start.5 = (s32[1024]{0:T(1024)S(1)}, s32[1024]{0:T(1024)}, u32[]{:S(2)}) copy-start(s32[1024]{0:T(1024)} %param.13) | copy-start | bytes 12292
  444.5 56.8 %all-gather.5.cloned.1.call-start = ((), (), s32[]{:S(2)}) async-start(), calls=%async_computation.5 | async-start | bytes 1179648 | tf_op jit(solution)/shard_map/all_gather | solution.py:46
  474.5 50.7 %all-to-all-start.1 = ((s32[64,1,2]{2,1,0:T(1,128)}), s32[64,1,2]{2,1,0:T(1,128)S(1)}, u32[]{:S(2)}, u32[]{:S(2)}) async-start(s32[64,1,2]{2,1,0:T(1,128)} %copy.50), calls=%async_computation.1 | async-start | bytes 65536 | tf_op jit(solution)/shard_map/all_to_all | solution.py:71
  525.1 15.8 %copy-start.1 = (bf16[1024,512]{0,1:T(8,128)(2,1)S(1)}, bf16[1024,512]{0,1:T(8,128)(2,1)}, u32[]{:S(2)}) copy-start(bf16[1024,512]{0,1:T(8,128)(2,1)} %all-gather.3.cloned.1.call-done) | copy-start | bytes 3145732
  525.1 15.8 %copy-start.2 = (bf16[1024,64]{0,1:T(8,128)(2,1)S(1)}, bf16[1024,64]{0,1:T(8,128)(2,1)}, u32[]{:S(2)}) copy-start(bf16[1024,64]{0,1:T(8,128)(2,1)} %get-tuple-element.3) | copy-start | bytes 393220
  525.2 302.4 %all-to-all-start.2 = ((bf16[64,2,128,64]{2,1,3,0:T(2,128)(2,1)}), bf16[64,2,128,64]{2,1,3,0:T(2,128)(2,1)}, u32[]{:S(2)}, u32[]{:S(2)}) async-start(bf16[64,2,128,64]{2,1,3,0:T(2,128)(2,1)} %copy.53), calls=%async_computation.2 | async-start | bytes 4194304 | tf_op jit(solution)/shard_map/all_to_all | solution.py:68
  540.9 285.1 %all-reduce.2.cloned.1.call-start = ((), (), s32[]{:S(2)}) async-start(), calls=%async_computation.4 | async-start | bytes 262144 | tf_op jit(solution)/shard_map/psum | solution.py:51
Sparse Core Ops, SparseCore 0:
  444.6 22.9 all-gather.2
  470.3 30.9 all-gather.4
  545.7 280.2 all-reduce.1
